TPU v7x, 512 devices: a whole 4x8x8 slice. The times are simulated.
512 devices in a mesh: row: 16 (over x, y_lo), col: 32 (over y_hi, z, core).
Axes of the slice: x: 4, y: 8 (y_hi: 2, y_lo: 4; y = y_hi * 4 + y_lo), z: 8, core: 2. Of those that a mesh axis runs over, the one named last changes fastest.
Arguments:
- bricks: bfloat16 [16, 32, 2, 16, 128, 128], P('row', 'col'), may hold values from -393216 to 393216
- brick_coords: int32 [16, 32, 3, 2], P('row', 'col'), may hold values from 0 to 31, as said below
- brick_counts: int32 [16, 32], P('row', 'col'), may hold values from 0 to 2, as said below
- step_sizes: float32 [2, 3], replicated, may hold values from 0.3 to 1
- init_a: float32 [16, 512, 256], P('row', 'col'), may hold values from -6 to 6
- init_b: float32 [32, 256, 256], P('col', 'row'), may hold values from -6 to 6
- init_c: float32 [512, 256], replicated, may hold values from -6 to 6
Outputs:
- factor_a: float32 [16, 512, 256], P('row', 'col')
- factor_b: float32 [32, 256, 256], P('col', 'row')
- factor_c: float32 [512, 256], replicated
Inputs may be any that keep to these rules, and one draw needn't show every extreme that they name: brick_counts of rows r and (r + half of the row axis) mod the row axis in one column add up to at most 3; some device holds 2 bricks. `brick_coords`: component 0 is below 4, component 1 below 2, component 2 below 32; dead slots hold arbitrary positions.
All inputs are finite; a program needn't handle non-finite values.
Results may differ from a plain program's by a relative error of at most 0.0003.
The roundings to bfloat16 on the way count: a program that leaves them out, or rounds other values in their place, can miss the bound.
Values may be sent and summed in bfloat16 or wider, within the bound.
No kernel may reach another device: no remote copies, remote signals or barrier semaphores. Data moves between devices by JAX's collectives and lax.ppermute only.
A program may use at most 64 MiB of HBM per device.

v0:
```python
import jax
import jax.numpy as jnp
from jax import lax
from jax.sharding import PartitionSpec as P


def brick_terms(brick, a_tile, b_tile, c_rows):
    depth, tile, _ = brick.shape
    wide = jnp.dot(
        brick.reshape(depth * tile, tile), b_tile, preferred_element_type=jnp.float32
    ).reshape(depth, tile, -1)
    c_wide = c_rows.astype(jnp.float32)[:, None, :]
    along_a = jnp.sum(wide * c_wide, axis=0)
    deep = jnp.einsum("kij,ir->kjr", brick, a_tile, preferred_element_type=jnp.float32)
    along_b = jnp.sum(deep * c_wide, axis=0)
    along_c = jnp.sum(deep * b_tile.astype(jnp.float32)[None, :, :], axis=1)
    return (along_a, along_b, along_c)


def add_tile(total, delta, start):
    old = lax.dynamic_slice_in_dim(total, start, delta.shape[0], 0)
    return lax.dynamic_update_slice_in_dim(total, old + delta, start, 0)


def gram(values):
    return jnp.dot(values.T, values, preferred_element_type=jnp.float32)


def project(state, hess, drive, rate):
    scale = jnp.sum(jnp.abs(hess), axis=1) + 1e-06
    slope = (
        jnp.dot(state, hess, precision=lax.Precision.HIGHEST, preferred_element_type=jnp.float32)
        - drive
    )
    return jnp.maximum(state - rate * slope / scale[None, :], 0.0)


def shards(bricks, brick_coords, brick_counts, step_sizes, init_a, init_b, init_c):
    slab = bricks[0, 0]
    places = brick_coords[0, 0]
    own = brick_counts[0, 0]
    depth = slab.shape[1]
    tile = slab.shape[2]
    sweeps = step_sizes.shape[0]
    state_a = init_a[0]
    state_b = init_b[0]
    state_c = init_c
    for sweep in range(sweeps):
        a_bf = state_a.astype(jnp.bfloat16)
        b_bf = state_b.astype(jnp.bfloat16)
        c_bf = state_c.astype(jnp.bfloat16)
        a_range = lax.all_gather(a_bf, "col", axis=0, tiled=True)
        b_range = lax.all_gather(b_bf, "row", axis=0, tiled=True)
        local_ga = gram(a_bf)
        local_gb = gram(b_bf)
        gram_a, gram_b = lax.psum((local_ga, local_gb), ("row", "col"))
        gram_c = gram(c_bf)

        def own_step(slot, carry):
            total_a, total_b, total_c = carry
            brick = lax.dynamic_index_in_dim(slab, slot, 0, keepdims=False)
            spot = lax.dynamic_index_in_dim(places, slot, 1, keepdims=False)
            i_low = spot[0] * tile
            j_low = spot[1] * tile
            k_low = spot[2] * depth
            a_tile = lax.dynamic_slice_in_dim(a_range, i_low, tile, 0)
            b_tile = lax.dynamic_slice_in_dim(b_range, j_low, tile, 0)
            c_rows = lax.dynamic_slice_in_dim(c_bf, k_low, depth, 0)
            delta_a, delta_b, delta_c = brick_terms(brick, a_tile, b_tile, c_rows)
            return (
                add_tile(total_a, delta_a, i_low),
                add_tile(total_b, delta_b, j_low),
                add_tile(total_c, delta_c, k_low),
            )

        empty = (
            jnp.zeros(a_range.shape, jnp.float32),
            jnp.zeros(b_range.shape, jnp.float32),
            jnp.zeros(c_bf.shape, jnp.float32),
        )
        drive_a, drive_b, drive_c = lax.fori_loop(0, own, own_step, empty)
        mine_a = lax.psum_scatter(drive_a, "col", scatter_dimension=0, tiled=True)
        mine_b = lax.psum_scatter(drive_b, "row", scatter_dimension=0, tiled=True)
        summed_c = lax.psum(drive_c, ("row", "col"))
        new_c = project(state_c, gram_a * gram_b, summed_c, step_sizes[sweep, 2])
        new_a = project(state_a, gram_b * gram_c, mine_a, step_sizes[sweep, 0])
        new_b = project(state_b, gram_a * gram_c, mine_b, step_sizes[sweep, 1])
        state_a, state_b, state_c = (new_a, new_b, new_c)
    return (state_a[None], state_b[None], state_c)


def solution(mesh):
    placed = (
        P("row", "col", None, None, None, None),
        P("row", "col", None, None),
        P("row", "col"),
        P(),
        P("row", "col", None),
        P("col", "row", None),
        P(),
    )
    return jax.shard_map(
        shards,
        mesh=mesh,
        in_specs=placed,
        out_specs=(P("row", "col", None), P("col", "row", None), P()),
        check_vma=False,
    )
```

profile of v0, /device:TPU:17, one launch (start us, length us, event | category | flops | bytes accessed | tf_op | source)
XLA Modules:
  0.0 791.6 jit_solution(12172388770690643116)
XLA Ops:
  8.1 1.7 fusion.61
  10.5 1.7 fusion.59
  13.0 31.3 %all_gather.12 = bf16[256,256]{1,0:T(8,128)(2,1)S(1)} all-gather(bf16[16,256]{1,0:T(8,128)(2,1)S(1)} %bitcast_convert_fusion), channel_id=1, replica_groups=mesh['row'=16,'col'=32] {'row'}, dimensions={0}, use_global_device_ids=true | all-gather | bytes 139264 | tf_op jit(solution)/shard_map/all_gather | solution.py:53
  44.3 65.9 %all_gather.13 = bf16[512,256]{1,0:T(8,128)(2,1)S(1)} all-gather(bf16[16,256]{1,0:T(8,128)(2,1)S(1)} %bitcast_convert_fusion.1), channel_id=1, replica_groups=mesh['row'=16,'col'=32] {'col'}, dimensions={0}, use_global_device_ids=true | all-gather | bytes 270336 | tf_op jit(solution)/shard_map/all_gather | solution.py:52
  110.4 6.1 while.28
  113.6 1.7 multiply_reduce_fusion.10
  116.5 1.0 copy.16
  119.6 275.4 %all-reduce.7.cloned.1.call-done = (f32[256,256]{1,0:T(8,128)}, f32[256,256]{1,0:T(8,128)}, f32[512,256]{0,1:T(8,128)}) async-done(((f32[256,256]{1,0:T(8,128)}, f32[256,256]{1,0:T(8,128)}, f32[512,256]{0,1:T(8,128)}), (f32[256,256]{1,0:T(8,128)}, f32[256,256]{1,0:T(8,128)}, f32[512,256]{0,1:T(8,128)})) %all-reduce.7.cloned.1.call-update) | async-done | bytes 1048592 | tf_op jit(solution)/shard_map/psum | solution.py:56
  395.1 1.5 abs_reduce_fusion.3
  396.6 1.7 fusion.69
  398.6 1.6 fusion.68
  400.2 29.4 %all_gather.14 = bf16[256,256]{1,0:T(8,128)(2,1)S(1)} all-gather(bf16[16,256]{1,0:T(8,128)(2,1)S(1)} %get-tuple-element.215), channel_id=1, replica_groups=mesh['row'=16,'col'=32] {'row'}, dimensions={0}, use_global_device_ids=true | all-gather | bytes 139264 | tf_op jit(solution)/shard_map/all_gather | solution.py:53
  430.5 1.6 fusion.70
  432.1 56.0 %all_gather.15 = bf16[512,256]{1,0:T(8,128)(2,1)S(1)} all-gather(bf16[16,256]{1,0:T(8,128)(2,1)S(1)} %get-tuple-element.219), channel_id=1, replica_groups=mesh['row'=16,'col'=32] {'col'}, dimensions={0}, use_global_device_ids=true | all-gather | bytes 270336 | tf_op jit(solution)/shard_map/all_gather | solution.py:52
  488.1 1.0 fusion.72
  489.2 6.2 while.29
  492.5 1.7 multiply_reduce_fusion.12
  495.4 1.0 copy.23
  497.8 277.9 %all-reduce.5.cloned.1.call-done = (f32[256,256]{1,0:T(8,128)}, f32[256,256]{1,0:T(8,128)}, f32[512,256]{0,1:T(8,128)}) async-done(((f32[256,256]{1,0:T(8,128)}, f32[256,256]{1,0:T(8,128)}, f32[512,256]{0,1:T(8,128)}), (f32[256,256]{1,0:T(8,128)}, f32[256,256]{1,0:T(8,128)}, f32[512,256]{0,1:T(8,128)})) %all-reduce.5.cloned.1.call-update) | async-done | bytes 1048592 | tf_op jit(solution)/shard_map/psum | solution.py:56
  775.7 1.5 abs_reduce_fusion
  777.3 1.4 fusion.30
  778.7 1.0 copy.25
  779.7 2.2 fusion.35
  781.9 2.1 fusion.40
  (82 shorter events, 8.6 us)
Async XLA Ops:
  8.0 36.3 %copy-start.4 = (f32[512,256]{1,0:T(8,128)S(1)}, f32[512,256]{1,0:T(8,128)}, u32[]{:S(2)}) copy-start(f32[512,256]{1,0:T(8,128)} %param.17) | copy-start | bytes 1572868
  8.0 387.1 %all-reduce.7.cloned.1.call-start = ((), (), s32[]{:S(2)}) async-start(), calls=%async_computation.9 | async-start | bytes 2097152 | tf_op jit(solution)/shard_map/psum | solution.py:56
  44.3 66.1 %copy-start.16 = (s32[1,1,3,2]{2,3,1,0:T(2,128)S(1)}, s32[1,1,3,2]{2,3,1,0:T(2,128)}, u32[]{:S(2)}) copy-start(s32[1,1,3,2]{2,3,1,0:T(2,128)} %param.12) | copy-start | bytes 76
  113.5 1.7 copy-start.13
  116.4 1.1 copy-start.1
  116.4 1.1 copy-start.3
  117.5 1.4 copy-start.12
  117.5 281.0 %reduce-scatter.7.cloned.1.call-start = ((), (), s32[]{:S(2)}) async-start(), calls=%async_computation.5 | async-start | bytes 278528 | tf_op jit(solution)/shard_map/reduce_scatter | solution.py:83
  118.1 312.4 %reduce-scatter.5.cloned.1.call-start = ((), (), s32[]{:S(2)}) async-start(), calls=%async_computation.4 | async-start | bytes 540672 | tf_op jit(solution)/shard_map/reduce_scatter | solution.py:82
  118.7 657.0 %all-reduce.5.cloned.1.call-start = ((), (), s32[]{:S(2)}) async-start(), calls=%async_computation.8 | async-start | bytes 2097152 | tf_op jit(solution)/shard_map/psum | solution.py:56
  395.1 1.5 copy-start.5
  395.1 1.5 copy-start.6
  395.1 1.5 copy-start.9
  396.6 2.0 copy-start.10
  398.4 32.1 %copy-start.11 = (f32[1,16,256]{2,1,0:T(8,128)S(1)}, f32[1,16,256]{2,1,0:T(8,128)}, u32[]{:S(2)}) copy-start(f32[1,16,256]{2,1,0:T(8,128)} %param.15) | copy-start | bytes 49156
  492.5 1.7 copy-start.14
  495.4 1.1 copy-start
  495.4 1.1 copy-start.2
  496.5 283.2 %reduce-scatter.11.cloned.1.call-start = ((), (), s32[]{:S(2)}) async-start(), calls=%async_computation.7 | async-start | bytes 278528 | tf_op jit(solution)/shard_map/reduce_scatter | solution.py:83
  497.1 284.8 %reduce-scatter.9.cloned.1.call-start = ((), (), s32[]{:S(2)}) async-start(), calls=%async_computation.6 | async-start | bytes 540672 | tf_op jit(solution)/shard_map/reduce_scatter | solution.py:82
  775.7 1.5 copy-start.7
  775.7 1.5 copy-start.8
  775.7 1.5 copy-start.15
Sparse Core Ops, SparseCore 0:
  117.6 277.4 all-reduce.6
  496.6 279.0 all-reduce.4
Sparse Core Ops, SparseCore 1:
  120.8 68.2 reduce-scatter.6
  193.5 133.6 reduce-scatter.4
  499.8 69.9 reduce-scatter.10
  574.3 133.7 reduce-scatter.8
where the time goes:
time: 793 us; the launch traced here: 792 us
  waiting for transfers between devices  556 us (70%)
  blocking collectives  183 us (23%)
  matrix products  23.2 us (3%)
  between operations  16 us (2%)
    psum x2, waiting for transfers between devices, shards(): gram_a, gram_b = lax.psum((local_ga, local_gb), ('row', 'col'))  553 us
    all_gather x2, blocking collectives, shards(): a_range = lax.all_gather(a_bf, 'col', axis=0, tiled=True)  122 us
    all_gather x2, blocking collectives, shards(): b_range = lax.all_gather(b_bf, 'row', axis=0, tiled=True)  60.7 us
  transfers between devices with their start and end apart: 6, of which 2 were waited for; matrix products, arithmetic and copies ran while one was open for 2% of the time, Pallas kernels for 0%

commit v1 on v0

--- a/solution.py
+++ b/solution.py
@@ -50,7 +50,9 @@
         b_bf = state_b.astype(jnp.bfloat16)
         c_bf = state_c.astype(jnp.bfloat16)
         a_range = lax.all_gather(a_bf, "col", axis=0, tiled=True)
-        b_range = lax.all_gather(b_bf, "row", axis=0, tiled=True)
+        b_range = jnp.concatenate(
+            lax.all_to_all(jnp.stack([b_bf] * lax.axis_size("row")), "row", 0, 0), axis=0
+        )
         local_ga = gram(a_bf)
         local_gb = gram(b_bf)
         gram_a, gram_b = lax.psum((local_ga, local_gb), ("row", "col"))

time: 793 us -> 734 us (0.926)
  blocking collectives: 183 us -> 110 us
  starting transfers between devices: 0.25 us -> 13.2 us
    all_gather x2 -> x0, blocking collectives: 60.7 us -> none  [shards(): b_range = lax.all_gather(b_bf, 'row', axis=0, tiled=True)]
    all_to_all x0 -> x2, starting transfers between devices: none -> 13 us  [shards(): lax.all_to_all(jnp.stack([b_bf] * lax.axis_size('row')), 'row', 0, 0)]
    all_gather x2, blocking collectives: 122 us -> 110 us  [shards(): a_range = lax.all_gather(a_bf, 'col', axis=0, tiled=True)]
  transfers between devices with their start and end apart: 6 -> 8, of which waited for: 2 -> 2; matrix products, arithmetic and copies ran while one was open for 2% -> 3% of each run, Pallas kernels for 0% -> 0%
where the time goes in v1:
time: 734 us; the launch traced here: 733 us
  waiting for transfers between devices  556 us (76%)
  blocking collectives  110 us (15%)
  matrix products  21.7 us (3%)
  between operations  16 us (2%)
  starting transfers between devices  13.2 us (2%)
    psum x2, waiting for transfers between devices, shards(): gram_a, gram_b = lax.psum((local_ga, local_gb), ('row', 'col'))  555 us
    all_gather x2, blocking collectives, shards(): a_range = lax.all_gather(a_bf, 'col', axis=0, tiled=True)  110 us
  transfers between devices with their start and end apart: 8, of which 2 were waited for; matrix products, arithmetic and copies ran while one was open for 3% of the time, Pallas kernels for 0%

profile of v1, /device:TPU:17, one launch (start us, length us, event | category | flops | bytes accessed | tf_op | source)
XLA Modules:
  0.0 732.6 jit_solution(461252400431646967)
XLA Ops:
  9.5 7.1 all-to-all-start
  16.6 0.9 fusion.68
  18.3 59.5 %all_gather.6 = bf16[512,256]{1,0:T(8,128)(2,1)S(1)} all-gather(bf16[16,256]{1,0:T(8,128)(2,1)S(1)} %bitcast_convert_fusion), channel_id=1, replica_groups=mesh['row'=16,'col'=32] {'col'}, dimensions={0}, use_global_device_ids=true | all-gather | bytes 270336 | tf_op jit(solution)/shard_map/all_gather | solution.py:52
  77.8 0.9 fusion.59
  78.8 6.1 while.28
  82.1 1.7 multiply_reduce_fusion.10
  85.0 1.0 copy.16
  87.6 276.8 %all-reduce.7.cloned.1.call-done = (f32[256,256]{1,0:T(8,128)}, f32[256,256]{1,0:T(8,128)}, f32[512,256]{0,1:T(8,128)}) async-done(((f32[256,256]{1,0:T(8,128)}, f32[256,256]{1,0:T(8,128)}, f32[512,256]{0,1:T(8,128)}), (f32[256,256]{1,0:T(8,128)}, f32[256,256]{1,0:T(8,128)}, f32[512,256]{0,1:T(8,128)})) %all-reduce.7.cloned.1.call-update) | async-done | bytes 1048592 | tf_op jit(solution)/shard_map/psum | solution.py:58
  364.4 1.5 abs_reduce_fusion.3
  366.0 1.7 fusion.66
  367.9 1.6 fusion.65
  370.2 5.8 all-to-all-start.1
  377.0 1.6 fusion.67
  378.6 50.6 %all_gather.7 = bf16[512,256]{1,0:T(8,128)(2,1)S(1)} all-gather(bf16[16,256]{1,0:T(8,128)(2,1)S(1)} %get-tuple-element.219), channel_id=1, replica_groups=mesh['row'=16,'col'=32] {'col'}, dimensions={0}, use_global_device_ids=true | all-gather | bytes 270336 | tf_op jit(solution)/shard_map/all_gather | solution.py:52
  429.2 0.9 fusion.70
  430.3 6.3 while.29
  433.7 1.7 multiply_reduce_fusion.12
  436.6 1.0 copy.23
  439.0 277.7 %all-reduce.5.cloned.1.call-done = (f32[256,256]{1,0:T(8,128)}, f32[256,256]{1,0:T(8,128)}, f32[512,256]{0,1:T(8,128)}) async-done(((f32[256,256]{1,0:T(8,128)}, f32[256,256]{1,0:T(8,128)}, f32[512,256]{0,1:T(8,128)}), (f32[256,256]{1,0:T(8,128)}, f32[256,256]{1,0:T(8,128)}, f32[512,256]{0,1:T(8,128)})) %all-reduce.5.cloned.1.call-update) | async-done | bytes 1048592 | tf_op jit(solution)/shard_map/psum | solution.py:58
  716.7 1.5 abs_reduce_fusion
  718.2 1.4 fusion.30
  719.6 1.0 copy.25
  720.6 2.2 fusion.35
  722.8 2.2 fusion.40
  (86 shorter events, 9.5 us)
Async XLA Ops:
  8.0 69.8 %copy-start.10 = (f32[1,16,256]{2,1,0:T(8,128)S(1)}, f32[1,16,256]{2,1,0:T(8,128)}, u32[]{:S(2)}) copy-start(f32[1,16,256]{2,1,0:T(8,128)} %param.15) | copy-start | bytes 49156
  8.0 69.7 %copy-start.4 = (f32[512,256]{1,0:T(8,128)S(1)}, f32[512,256]{1,0:T(8,128)}, u32[]{:S(2)}) copy-start(f32[512,256]{1,0:T(8,128)} %param.17) | copy-start | bytes 1572868
  9.5 69.3 %all-to-all-start = ((bf16[16,16,256]{2,1,0:T(8,128)(2,1)}), bf16[16,16,256]{2,1,0:T(8,128)(2,1)S(1)}, u32[]{:S(2)}, u32[]{:S(2)}) async-start(bf16[16,16,256]{2,1,0:T(8,128)(2,1)} %stack.4), calls=%async_computation | async-start | bytes 262144 | tf_op jit(solution)/shard_map/all_to_all | solution.py:54
  16.6 347.8 %all-reduce.7.cloned.1.call-start = ((), (), s32[]{:S(2)}) async-start(), calls=%async_computation.11 | async-start | bytes 2097152 | tf_op jit(solution)/shard_map/psum | solution.py:58
  77.7 1.1 copy-start.16
  82.1 1.7 copy-start.13
  85.0 1.1 copy-start.1
  85.0 1.1 copy-start.3
  86.1 281.8 %reduce-scatter.7.cloned.1.call-start = ((), (), s32[]{:S(2)}) async-start(), calls=%async_computation.7 | async-start | bytes 278528 | tf_op jit(solution)/shard_map/reduce_scatter | solution.py:85
  86.7 290.3 %reduce-scatter.5.cloned.1.call-start = ((), (), s32[]{:S(2)}) async-start(), calls=%async_computation.6 | async-start | bytes 540672 | tf_op jit(solution)/shard_map/reduce_scatter | solution.py:84
  364.4 1.5 copy-start.5
  364.4 1.5 copy-start.6
  364.4 1.5 copy-start.9
  365.9 1.9 copy-start.11
  370.2 60.0 %all-to-all-start.1 = ((bf16[16,16,256]{2,1,0:T(8,128)(2,1)}), bf16[16,16,256]{2,1,0:T(8,128)(2,1)S(1)}, u32[]{:S(2)}, u32[]{:S(2)}) async-start(bf16[16,16,256]{2,1,0:T(8,128)(2,1)} %stack.5), calls=%async_computation.3 | async-start | bytes 262144 | tf_op jit(solution)/shard_map/all_to_all | solution.py:54
  376.0 340.7 %all-reduce.5.cloned.1.call-start = ((), (), s32[]{:S(2)}) async-start(), calls=%async_computation.10 | async-start | bytes 2097152 | tf_op jit(solution)/shard_map/psum | solution.py:58
  433.7 1.7 copy-start.14
  436.6 1.1 copy-start
  436.6 1.1 copy-start.2
  437.7 283.0 %reduce-scatter.11.cloned.1.call-start = ((), (), s32[]{:S(2)}) async-start(), calls=%async_computation.9 | async-start | bytes 278528 | tf_op jit(solution)/shard_map/reduce_scatter | solution.py:85
  438.2 284.6 %reduce-scatter.9.cloned.1.call-start = ((), (), s32[]{:S(2)}) async-start(), calls=%async_computation.8 | async-start | bytes 540672 | tf_op jit(solution)/shard_map/reduce_scatter | solution.py:84
  716.7 1.5 copy-start.7
  716.7 1.5 copy-start.8
  716.7 1.5 copy-start.15
  (1 other events, 0.9 us)
Sparse Core Ops, SparseCore 0:
  86.2 278.1 all-reduce.6
  437.8 278.8 all-reduce.4
Sparse Core Ops, SparseCore 1:
  89.3 68.7 reduce-scatter.6
  162.5 133.7 reduce-scatter.4
  440.9 69.3 reduce-scatter.10
  514.9 134.1 reduce-scatter.8
